TPU v7x, 32 devices: a whole 2x2x4 slice. The times are simulated.
32 devices in a mesh: groups: 2 (over y), tok: 4 (over z), slot: 2 (over x), hid: 2 (over core).
Axes of the slice: x: 2, y: 2, z: 4, core: 2. Of those that a mesh axis runs over, the one named last changes fastest.
Arguments:
- tokens: bfloat16 [8192, 1024], P(('groups', 'tok', 'slot', 'hid')), parts along dimension 0, may hold values from -12 to 12
- slot_keys: bfloat16 [2048, 512], P('groups', 'slot'), parts along dimension 0, may hold values from -12 to 12
- w_in: bfloat16 [4, 4, 1024, 4096], P(('groups', 'slot'), 'tok', None, 'hid'), parts along dimension 0, may hold values from -0.1875 to 0.1875
- w_out: bfloat16 [4, 4, 4096, 1024], P(('groups', 'slot'), 'tok', 'hid'), parts along dimension 0, may hold values from -0.09375 to 0.09375
Outputs:
- mixed: float32 [8192, 1024], P(('groups', 'tok', 'slot', 'hid')), parts along dimension 0
There are 2 independent parts, one for each index of `groups`. A program takes and returns all parts, laid end to end along the dimension named above; each array names one. Nothing has to cross between parts.
All inputs are finite; a program needn't handle non-finite values.
Results may differ from a plain program's by a relative error of at most 0.0022.
Values may be sent and summed in bfloat16 or wider, within the bound.
No kernel may reach another device: no remote copies, remote signals or barrier semaphores. Data moves between devices by JAX's collectives and lax.ppermute only.
A program may use at most 64 MiB of HBM per device.

v0:
```python
import jax
import jax.numpy as jnp
from jax import lax
from jax.sharding import PartitionSpec as P

epsilon = 1e-06


def local(tokens, slot_keys, w_in, w_out):
    model_width = tokens.shape[1]
    block_width = slot_keys.shape[1]
    owned_slots = block_width // (lax.axis_size("tok") * lax.axis_size("hid"))
    key_scale = lax.rsqrt(jnp.mean(jnp.square(slot_keys.astype(jnp.float32)), axis=0) + epsilon)
    fragment = lax.all_gather(tokens, "slot", axis=0, tiled=True)
    token_scale = lax.rsqrt(jnp.mean(jnp.square(fragment.astype(jnp.float32)), axis=1) + epsilon)
    logits = (
        4.0
        * token_scale[:, None]
        * key_scale[None, :]
        * jnp.dot(fragment, slot_keys, preferred_element_type=jnp.float32)
        / model_width
    )
    weights_exp = jnp.exp(logits)
    weights_low = weights_exp.astype(jnp.bfloat16)
    slot_numer = lax.dot_general(
        weights_low, fragment, (((0,), (0,)), ((), ())), preferred_element_type=jnp.float32
    )
    slot_denom = jnp.sum(weights_exp, axis=0)
    weights_all = weights_low
    token_denom = jnp.sum(weights_exp, axis=1)
    slot_numer, slot_denom, weights_all, token_denom = (
        slot_numer,
        slot_denom,
        weights_all,
        token_denom,
    )
    summed_numer, summed_denom = lax.psum((slot_numer, slot_denom), ("tok", "hid"))
    first_slot = lax.axis_index(("tok", "hid")) * owned_slots
    owned_numer = lax.dynamic_slice_in_dim(summed_numer, first_slot, owned_slots, 0)
    owned_denom = lax.dynamic_slice_in_dim(summed_denom, first_slot, owned_slots, 0)
    owned_inputs = (owned_numer / owned_denom[:, None]).astype(jnp.bfloat16)
    expert_inputs = lax.all_gather(owned_inputs, "hid", axis=0, tiled=True)
    hidden = jax.nn.gelu(
        jnp.dot(expert_inputs, w_in[0, 0], preferred_element_type=jnp.float32), approximate=True
    ).astype(jnp.bfloat16)
    half_outputs = jnp.dot(hidden, w_out[0, 0], preferred_element_type=jnp.float32)
    owned_outputs = lax.psum_scatter(half_outputs, "hid", scatter_dimension=0, tiled=True).astype(
        jnp.bfloat16
    )
    block_outputs = lax.all_gather(owned_outputs, ("tok", "hid"), axis=0, tiled=True)
    token_numer = jnp.dot(weights_all, block_outputs, preferred_element_type=jnp.float32)
    mine_numer, mine_denom = (
        lax.psum_scatter(token_numer, "slot", scatter_dimension=0, tiled=True),
        lax.psum_scatter(token_denom, "slot", scatter_dimension=0, tiled=True),
    )
    return mine_numer / mine_denom[:, None]


def solution(mesh):
    in_specs = (
        P(("groups", "tok", "slot", "hid"), None),
        P("groups", "slot"),
        P(("groups", "slot"), "tok", None, "hid"),
        P(("groups", "slot"), "tok", "hid", None),
    )
    out_specs = P(("groups", "tok", "slot", "hid"), None)
    return jax.shard_map(local, mesh=mesh, in_specs=in_specs, out_specs=out_specs, check_vma=False)
```

profile of v0, /device:TPU:0, one launch (start us, length us, event | category | flops | bytes accessed | tf_op | source)
XLA Modules:
  0.0 172.2 jit_solution(18349934714928174129)
XLA Ops:
  6.5 0.0 all-gather.2.cloned.1.call-start
  6.5 0.7 all-gather.2.cloned.1.call-update
  7.3 0.0 all-reduce.3.cloned.1.call-start
  7.3 1.2 multiply_reduce_fusion.1
  8.5 24.4 %all-gather.2.cloned.1.call-done = bf16[512,1024]{1,0:T(8,128)(2,1)} async-done(((bf16[256,1024]{1,0:T(8,128)(2,1)}), bf16[512,1024]{1,0:T(8,128)(2,1)}) %all-gather.2.cloned.1.call-update) | async-done | bytes 1048592 | tf_op jit(solution)/shard_map/all_gather | solution.py:14
  32.9 0.0 copy-start
  32.9 1.6 multiply_reduce_fusion
  34.5 1.9 %fusion.32 = (f32[512]{0:T(512)S(1)}, f32[256]{0:T(256)S(1)}, bf16[512,256]{1,0:T(8,128)(2,1)S(1)}) fusion(bf16[512,1024]{1,0:T(8,128)(2,1)} %all-gather.2.cloned.1.call-done, bf16[1024,256]{1,0:T(8,128)(2,1)} %param.5, f32[256]{0:T(256)S(1)} %add_rsqrt_fusion, f32[512]{0:T(512)S(1)} %rsqrt_multiply_fusion), kind=kOutput, calls=%fused_computation.34 | convolution fusion | flops 269221120 | bytes 1841152 | tf_op jit(solution)/shard_map/dot_general | solution.py:20
  36.4 0.0 copy-done
  36.4 1.4 fusion.26
  37.9 0.0 all-reduce.3.cloned.1.call-update
  37.9 0.0 reduce-scatter.3.cloned.1.call-start
  38.0 16.4 %psum.15 = f32[256]{0:T(256)S(1)} all-reduce(f32[256]{0:T(256)S(1)} %get-tuple-element.6), channel_id=1, replica_groups=mesh['groups'=2,'tok'=4,'slot'=2,'hid'=2] {'tok','hid'}, use_global_device_ids=true, to_apply=%region_4.0 | all-reduce | flops 256 | bytes 2048 | tf_op jit(solution)/shard_map/psum | solution.py:37
  54.4 0.1 dynamic_slice.7
  54.5 42.5 %all-reduce.3.cloned.1.call-done = f32[256,1024]{1,0:T(8,128)} async-done(((f32[256,1024]{1,0:T(8,128)}), f32[256,1024]{1,0:T(8,128)}) %all-reduce.3.cloned.1.call-update) | async-done | bytes 1048592 | tf_op jit(solution)/shard_map/psum | solution.py:37
  97.0 1.0 divide_convert_fusion
  98.0 1.9 %all_gather.10 = bf16[64,1024]{1,0:T(8,128)(2,1)S(1)} all-gather(bf16[32,1024]{1,0:T(8,128)(2,1)S(1)} %divide_convert_fusion), channel_id=1, replica_groups=mesh['groups'=2,'tok'=4,'slot'=2,'hid'=2] {'hid'}, dimensions={0}, use_global_device_ids=true | all-gather | bytes 196608 | tf_op jit(solution)/shard_map/all_gather | solution.py:42
  99.9 5.9 %fusion = f32[64,1024]{1,0:T(8,128)} fusion(bf16[1,1,2048,1024]{3,2,1,0:T(8,128)(2,1)} %param.7, bf16[64,1024]{1,0:T(8,128)(2,1)S(1)} %all_gather.10, bf16[1,1,1024,2048]{3,2,1,0:T(8,128)(2,1)} %param.6), kind=kOutput, calls=%fused_computation | convolution fusion | flops 538050560 | bytes 8781824 | tf_op jit(solution)/shard_map/dot_general | solution.py:46
  105.7 0.0 copy-start.1
  105.7 0.0 reduce-scatter.3.cloned.1.call-update
  105.7 0.0 reduce-scatter.5.cloned.1.call-start
  105.8 6.7 %reduce-scatter.3.cloned.1.call-done = f32[32,1024]{1,0:T(8,128)} async-done(((f32[64,1024]{1,0:T(8,128)}), f32[32,1024]{1,0:T(8,128)}) %reduce-scatter.3.cloned.1.call-update) | async-done | bytes 131088 | tf_op jit(solution)/shard_map/reduce_scatter | solution.py:47
  112.5 0.9 convert_element_type.23
  113.4 15.0 %all_gather.11 = bf16[256,1024]{1,0:T(8,128)(2,1)S(1)} all-gather(bf16[32,1024]{1,0:T(8,128)(2,1)S(1)} %convert_element_type.23), channel_id=1, replica_groups=mesh['groups'=2,'tok'=4,'slot'=2,'hid'=2] {'tok','hid'}, dimensions={0}, use_global_device_ids=true | all-gather | bytes 589824 | tf_op jit(solution)/shard_map/all_gather | solution.py:50
  128.4 1.8 %fusion.24 = f32[512,1024]{1,0:T(8,128)} fusion(bf16[256,1024]{1,0:T(8,128)(2,1)S(1)} %all_gather.11, bf16[512,256]{1,0:T(8,128)(2,1)S(1)} %get-tuple-element.7), kind=kOutput, calls=%fused_computation.24 | convolution fusion | flops 268435456 | bytes 2883584 | tf_op jit(solution)/shard_map/dot_general | solution.py:51
  130.2 0.0 reduce-scatter.5.cloned.1.call-update
  130.2 0.0 copy-done.1
  130.3 0.6 dynamic-slice
  131.5 4.9 %all-reduce = f32[512]{0:T(512)S(1)} all-reduce(f32[512]{0:T(512)S(1)} %get-tuple-element.5), channel_id=4, replica_groups=mesh['groups'=2,'tok'=4,'slot'=2,'hid'=2] {'slot'}, use_global_device_ids=true, to_apply=%region_8.0.clone | all-reduce | flops 512 | bytes 4096
  136.4 0.1 dynamic-slice.1
  136.5 26.8 %reduce-scatter.5.cloned.1.call-done = f32[256,1024]{1,0:T(8,128)} async-done(((f32[512,1024]{1,0:T(8,128)}), f32[256,1024]{1,0:T(8,128)}) %reduce-scatter.5.cloned.1.call-update) | async-done | bytes 1048592 | tf_op jit(solution)/shard_map/reduce_scatter | solution.py:53
  163.3 2.3 %broadcast_divide_fusion = f32[256,1024]{1,0:T(8,128)} fusion(f32[256,1024]{1,0:T(8,128)} %reduce-scatter.5.cloned.1.call-done, f32[256]{0:T(256)S(1)} %dynamic-slice.1), kind=kLoop, calls=%fused_computation.18 | loop fusion | flops 262144 | bytes 2098176 | tf_op jit(solution)/shard_map/div | solution.py:56
  (2 shorter events, 0.0 us)
Async XLA Ops:
  6.5 26.4 %all-gather.2.cloned.1.call-start = ((), (), s32[]{:S(2)}) async-start(), calls=%async_computation.2 | async-start | bytes 1572864 | tf_op jit(solution)/shard_map/all_gather | solution.py:14
  7.3 89.7 %all-reduce.3.cloned.1.call-start = ((), (), s32[]{:S(2)}) async-start(), calls=%async_computation.3 | async-start | bytes 2097152 | tf_op jit(solution)/shard_map/psum | solution.py:37
  32.9 3.5 %copy-start = (bf16[512,1024]{1,0:T(8,128)(2,1)S(1)}, bf16[512,1024]{1,0:T(8,128)(2,1)}, u32[]{:S(2)}) copy-start(bf16[512,1024]{1,0:T(8,128)(2,1)} %all-gather.2.cloned.1.call-done) | copy-start | bytes 3145732
  37.9 74.6 %reduce-scatter.3.cloned.1.call-start = ((), (), s32[]{:S(2)}) async-start(), calls=%async_computation.4 | async-start | bytes 393216 | tf_op jit(solution)/shard_map/reduce_scatter | solution.py:47
  105.7 24.5 %copy-start.1 = (u32[32]{0:T(128)S(1)}, u32[32]{0:T(128)}, u32[]{:S(2)}) copy-start(u32[32]{0:T(128)} %constant.43) | copy-start | bytes 388
  105.7 57.6 %reduce-scatter.5.cloned.1.call-start = ((), (), s32[]{:S(2)}) async-start(), calls=%async_computation.5 | async-start | bytes 3145728 | tf_op jit(solution)/shard_map/reduce_scatter | solution.py:53
Sparse Core Ops, SparseCore 0:
  8.9 23.9 all-gather.1
  38.0 58.8 all-reduce.2
  105.9 6.6 reduce-scatter.2
  130.4 32.8 reduce-scatter.4
where the time goes:
time: 173 us; the launch traced here: 172 us
  waiting for transfers between devices  101 us (58%)
  blocking collectives  38.2 us (22%)
  between operations  13.8 us (8%)
  matrix products  11 us (6%)
  other arithmetic  7.06 us (4%)
    psum x1, waiting for transfers between devices, local(): lax.psum((slot_numer, slot_denom), ('tok', 'hid'))  42.5 us
    reduce_scatter x1, waiting for transfers between devices, local(): lax.psum_scatter(token_numer, 'slot', scatter_dimension=0, tiled=True)  26.8 us
    all_gather x1, waiting for transfers between devices, local(): fragment = lax.all_gather(tokens, 'slot', axis=0, tiled=True)  24.4 us
    psum x1, blocking collectives, local(): lax.psum((slot_numer, slot_denom), ('tok', 'hid'))  16.4 us
    all_gather x1, blocking collectives, local(): lax.all_gather(owned_outputs, ('tok', 'hid'), axis=0, tiled=True)  15 us
    reduce_scatter x1, waiting for transfers between devices, local(): lax.psum_scatter(half_outputs, 'hid', scatter_dimension=0, tiled=True)  6.72 us
    dot_general x1, matrix products, local(): jnp.dot(hidden, w_out[0, 0], preferred_element_type=jnp.float32)  5.86 us
    unnamed x1, blocking collectives  4.94 us
  transfers between devices with their start and end apart: 4, of which 4 were waited for; matrix products, arithmetic and copies ran while one was open for 1% of the time, Pallas kernels for 0%

commit v1 on v0

--- a/solution.py
+++ b/solution.py
@@ -1,9 +1,43 @@
+import functools
 import jax
 import jax.numpy as jnp
 from jax import lax
 from jax.sharding import PartitionSpec as P
 
 epsilon = 1e-06
+
+
+def fit_loops(vec, dim_at):
+    z = list(vec.shape[1:])
+    z[dim_at] *= vec.shape[0]
+    return jnp.moveaxis(vec, 0, dim_at).reshape(z)
+
+
+def connect_lanes_for(x_local, mesh_dim, k_dim):
+    n_axis = lax.axis_size(mesh_dim)
+    so_far_all = []
+    for dev_j in range(n_axis):
+        so_far_all.append((dev_j, (dev_j + 1) % n_axis))
+    buffers = []
+    for d, b in so_far_all:
+        buffers.append((b, d))
+    odd, after = ([], [])
+    for h in range(n_axis - 1):
+        if h % 2 == 0:
+            lower = lax.ppermute(odd[-1] if odd else x_local, mesh_dim, so_far_all)
+            odd.append(lower)
+        else:
+            met_up = lax.ppermute(after[-1] if after else x_local, mesh_dim, perm=buffers)
+            after.append(met_up)
+    back = jnp.stack([*odd[::-1], x_local, *after])
+    o_now = lax.axis_index(mesh_dim)
+    s_next = len(odd)
+    piece_next = o_now - s_next
+    back = back[(jnp.arange(n_axis) - piece_next) % n_axis]
+    return fit_loops(back, k_dim)
+
+
+carry_seats_all = functools.partial(connect_lanes_for, mesh_dim=("tok", "hid"), k_dim=0)
 
 
 def local(tokens, slot_keys, w_in, w_out):
@@ -47,7 +81,7 @@
     owned_outputs = lax.psum_scatter(half_outputs, "hid", scatter_dimension=0, tiled=True).astype(
         jnp.bfloat16
     )
-    block_outputs = lax.all_gather(owned_outputs, ("tok", "hid"), axis=0, tiled=True)
+    block_outputs = carry_seats_all(owned_outputs)
     token_numer = jnp.dot(weights_all, block_outputs, preferred_element_type=jnp.float32)
     mine_numer, mine_denom = (
         lax.psum_scatter(token_numer, "slot", scatter_dimension=0, tiled=True),

time: 173 us -> 181 us (1.046)
  blocking collectives: 38.2 us -> 23.3 us
  waiting for transfers between devices: 101 us -> 112 us
  starting transfers between devices: 0.12 us -> 11.1 us
    all_gather x1 -> x0, blocking collectives: 15 us -> none  [local(): lax.all_gather(owned_outputs, ('tok', 'hid'), axis=0, tiled=True)]
    ppermute x0 -> x7, waiting for transfers between devices: none -> 11.5 us  [the longest x4 11.5 us: connect_lanes_for(): lower = lax.ppermute(odd[-1] if odd else x_local, mesh_dim, so_far_all)]
    ppermute x0 -> x7, starting transfers between devices: none -> 11 us  [the longest x3 10.7 us: connect_lanes_for(): lax.ppermute(after[-1] if after else x_local, mesh_dim, perm=buffers)]
  transfers between devices with their start and end apart: 4 -> 11, of which waited for: 4 -> 8; matrix products, arithmetic and copies ran while one was open for 1% -> 2% of each run, Pallas kernels for 0% -> 0%
where the time goes in v1:
time: 181 us
  waiting for transfers between devices  112 us (62%)
  blocking collectives  23.3 us (13%)
  between operations  13.9 us (8%)
  starting transfers between devices  11.1 us (6%)
  matrix products  11 us (6%)
  other arithmetic  8 us (4%)
    psum x1, waiting for transfers between devices, local(): lax.psum((slot_numer, slot_denom), ('tok', 'hid'))  42.5 us
    reduce_scatter x1, waiting for transfers between devices, local(): lax.psum_scatter(token_numer, 'slot', scatter_dimension=0, tiled=True)  26.5 us
    all_gather x1, waiting for transfers between devices, local(): fragment = lax.all_gather(tokens, 'slot', axis=0, tiled=True)  24.4 us
    psum x1, blocking collectives, local(): lax.psum((slot_numer, slot_denom), ('tok', 'hid'))  16.4 us
    ppermute x4, waiting for transfers between devices, connect_lanes_for(): lower = lax.ppermute(odd[-1] if odd else x_local, mesh_dim, so_far_all)  11.5 us
    ppermute x3, starting transfers between devices, connect_lanes_for(): lax.ppermute(after[-1] if after else x_local, mesh_dim, perm=buffers)  10.7 us
    reduce_scatter x1, waiting for transfers between devices, local(): lax.psum_scatter(half_outputs, 'hid', scatter_dimension=0, tiled=True)  6.72 us
    dot_general x1, matrix products, local(): jnp.dot(hidden, w_out[0, 0], preferred_element_type=jnp.float32)  5.86 us
  transfers between devices with their start and end apart: 11, of which 8 were waited for; matrix products, arithmetic and copies ran while one was open for 2% of the time, Pallas kernels for 0%

profile of v1, /device:TPU:0, one launch (start us, length us, event | category | flops | bytes accessed | tf_op | source)
XLA Modules:
  0.0 180.9 jit_solution(279190170544671520)
XLA Ops:
  6.5 0.7 all-gather.2.cloned.1.call-update
  7.3 1.2 multiply_reduce_fusion.1
  8.5 24.4 %all-gather.2.cloned.1.call-done = bf16[512,1024]{1,0:T(8,128)(2,1)} async-done(((bf16[256,1024]{1,0:T(8,128)(2,1)}), bf16[512,1024]{1,0:T(8,128)(2,1)}) %all-gather.2.cloned.1.call-update) | async-done | bytes 1048592 | tf_op jit(solution)/shard_map/all_gather | solution.py:48
  32.9 1.6 multiply_reduce_fusion
  34.5 1.9 %fusion.34 = (f32[512]{0:T(512)S(1)}, f32[256]{0:T(256)S(1)}, bf16[512,256]{1,0:T(8,128)(2,1)S(1)}) fusion(bf16[512,1024]{1,0:T(8,128)(2,1)} %all-gather.2.cloned.1.call-done, bf16[1024,256]{1,0:T(8,128)(2,1)} %param.5, f32[256]{0:T(256)S(1)} %add_rsqrt_fusion, f32[512]{0:T(512)S(1)} %rsqrt_multiply_fusion), kind=kOutput, calls=%fused_computation.50 | convolution fusion | flops 269221120 | bytes 1841152 | tf_op jit(solution)/shard_map/dot_general | solution.py:54
  36.4 1.4 fusion.26
  37.9 0.0 reduce-scatter.3.cloned.1.call-start
  38.0 16.4 %psum.15 = f32[256]{0:T(256)S(1)} all-reduce(f32[256]{0:T(256)S(1)} %get-tuple-element.6), channel_id=1, replica_groups=mesh['groups'=2,'tok'=4,'slot'=2,'hid'=2] {'tok','hid'}, use_global_device_ids=true, to_apply=%region_4.0 | all-reduce | flops 256 | bytes 2048 | tf_op jit(solution)/shard_map/psum | solution.py:71
  54.4 0.1 dynamic_slice.7
  54.5 42.5 %all-reduce.3.cloned.1.call-done = f32[256,1024]{1,0:T(8,128)} async-done(((f32[256,1024]{1,0:T(8,128)}), f32[256,1024]{1,0:T(8,128)}) %all-reduce.3.cloned.1.call-update) | async-done | bytes 1048592 | tf_op jit(solution)/shard_map/psum | solution.py:71
  97.0 1.0 divide_convert_fusion
  98.0 1.9 %all_gather.7 = bf16[64,1024]{1,0:T(8,128)(2,1)S(1)} all-gather(bf16[32,1024]{1,0:T(8,128)(2,1)S(1)} %divide_convert_fusion), channel_id=1, replica_groups=mesh['groups'=2,'tok'=4,'slot'=2,'hid'=2] {'hid'}, dimensions={0}, use_global_device_ids=true | all-gather | bytes 196608 | tf_op jit(solution)/shard_map/all_gather | solution.py:76
  99.9 5.9 %fusion = f32[64,1024]{1,0:T(8,128)} fusion(bf16[1,1,2048,1024]{3,2,1,0:T(8,128)(2,1)} %param.7, bf16[64,1024]{1,0:T(8,128)(2,1)S(1)} %all_gather.7, bf16[1,1,1024,2048]{3,2,1,0:T(8,128)(2,1)} %param.6), kind=kOutput, calls=%fused_computation.1 | convolution fusion | flops 538050560 | bytes 8781824 | tf_op jit(solution)/shard_map/dot_general | solution.py:80
  105.7 0.0 reduce-scatter.5.cloned.1.call-start
  105.8 6.7 %reduce-scatter.3.cloned.1.call-done = f32[32,1024]{1,0:T(8,128)} async-done(((f32[64,1024]{1,0:T(8,128)}), f32[32,1024]{1,0:T(8,128)}) %reduce-scatter.3.cloned.1.call-update) | async-done | bytes 131088 | tf_op jit(solution)/shard_map/reduce_scatter | solution.py:81
  112.5 0.9 convert_element_type.23
  113.4 0.2 collective-permute-start
  113.7 5.3 %collective-permute-done = bf16[32,1024]{1,0:T(8,128)(2,1)S(1)} collective-permute-done((bf16[32,1024]{1,0:T(8,128)(2,1)S(1)}, bf16[32,1024]{1,0:T(8,128)(2,1)S(1)}, u32[]{:S(2)}, u32[]{:S(2)}) %collective-permute-start) | collective-permute-done | bytes 65568 | tf_op jit(solution)/shard_map/ppermute | solution.py:27
  119.0 3.5 %collective-permute-start.4 = (bf16[32,1024]{1,0:T(8,128)(2,1)S(1)}, bf16[32,1024]{1,0:T(8,128)(2,1)S(1)}, u32[]{:S(2)}, u32[]{:S(2)}) collective-permute-start(bf16[32,1024]{1,0:T(8,128)(2,1)S(1)} %convert_element_type.23), channel_id=1, source_target_pairs={{1,0},{4,1},{5,4},{8,5},{9,8},{12,9},{13,12},{0,13},{3,2},{6,3},{7... | collective-permute-start | bytes 196616 | tf_op jit(solution)/shard_map/ppermute | solution.py:30
  122.5 2.4 %collective-permute-done.1 = bf16[32,1024]{1,0:T(8,128)(2,1)S(1)} collective-permute-done((bf16[32,1024]{1,0:T(8,128)(2,1)S(1)}, bf16[32,1024]{1,0:T(8,128)(2,1)S(1)}, u32[]{:S(2)}, u32[]{:S(2)}) %collective-permute-start.1) | collective-permute-done | bytes 65568 | tf_op jit(solution)/shard_map/ppermute | solution.py:27
  124.9 3.6 %collective-permute-start.5 = (bf16[32,1024]{1,0:T(8,128)(2,1)S(1)}, bf16[32,1024]{1,0:T(8,128)(2,1)S(1)}, u32[]{:S(2)}, u32[]{:S(2)}) collective-permute-start(bf16[32,1024]{1,0:T(8,128)(2,1)S(1)} %collective-permute-done.4), channel_id=1, source_target_pairs={{1,0},{4,1},{5,4},{8,5},{9,8},{12,9},{13,12},{0,13},{3,2},{6,3},{7... | collective-permute-start | bytes 196616 | tf_op jit(solution)/shard_map/ppermute | solution.py:30
  128.5 1.9 %collective-permute-done.2 = bf16[32,1024]{1,0:T(8,128)(2,1)S(1)} collective-permute-done((bf16[32,1024]{1,0:T(8,128)(2,1)S(1)}, bf16[32,1024]{1,0:T(8,128)(2,1)S(1)}, u32[]{:S(2)}, u32[]{:S(2)}) %collective-permute-start.2) | collective-permute-done | bytes 65568 | tf_op jit(solution)/shard_map/ppermute | solution.py:27
  130.4 3.6 %collective-permute-start.6 = (bf16[32,1024]{1,0:T(8,128)(2,1)S(1)}, bf16[32,1024]{1,0:T(8,128)(2,1)S(1)}, u32[]{:S(2)}, u32[]{:S(2)}) collective-permute-start(bf16[32,1024]{1,0:T(8,128)(2,1)S(1)} %collective-permute-done.5), channel_id=1, source_target_pairs={{1,0},{4,1},{5,4},{8,5},{9,8},{12,9},{13,12},{0,13},{3,2},{6,3},{7... | collective-permute-start | bytes 196616 | tf_op jit(solution)/shard_map/ppermute | solution.py:30
  134.0 1.9 %collective-permute-done.3 = bf16[32,1024]{1,0:T(8,128)(2,1)S(1)} collective-permute-done((bf16[32,1024]{1,0:T(8,128)(2,1)S(1)}, bf16[32,1024]{1,0:T(8,128)(2,1)S(1)}, u32[]{:S(2)}, u32[]{:S(2)}) %collective-permute-start.3) | collective-permute-done | bytes 65568 | tf_op jit(solution)/shard_map/ppermute | solution.py:27
  136.0 0.9 bitcast_dynamic-update-slice_fusion.3
  136.9 0.6 gather_fusion
  137.5 1.8 fusion.24
  139.3 0.6 dynamic-slice
  140.6 4.9 %all-reduce = f32[512]{0:T(512)S(1)} all-reduce(f32[512]{0:T(512)S(1)} %get-tuple-element.5), channel_id=4, replica_groups=mesh['groups'=2,'tok'=4,'slot'=2,'hid'=2] {'slot'}, use_global_device_ids=true, to_apply=%region_8.9.clone | all-reduce | flops 512 | bytes 4096
  145.5 0.1 dynamic-slice.1
  145.6 26.5 %reduce-scatter.5.cloned.1.call-done = f32[256,1024]{1,0:T(8,128)} async-done(((f32[512,1024]{1,0:T(8,128)}), f32[256,1024]{1,0:T(8,128)}) %reduce-scatter.5.cloned.1.call-update) | async-done | bytes 1048592 | tf_op jit(solution)/shard_map/reduce_scatter | solution.py:87
  172.0 2.3 %broadcast_divide_fusion = f32[256,1024]{1,0:T(8,128)} fusion(f32[256,1024]{1,0:T(8,128)} %reduce-scatter.5.cloned.1.call-done, f32[256]{0:T(256)S(1)} %dynamic-slice.1), kind=kLoop, calls=%fused_computation.19 | loop fusion | flops 262144 | bytes 2098176 | tf_op jit(solution)/shard_map/div | solution.py:90
  (26 shorter events, 0.2 us)
Async XLA Ops:
  6.5 26.4 %all-gather.2.cloned.1.call-start = ((), (), s32[]{:S(2)}) async-start(), calls=%async_computation.2 | async-start | bytes 1572864 | tf_op jit(solution)/shard_map/all_gather | solution.py:48
  7.3 89.7 %all-reduce.3.cloned.1.call-start = ((), (), s32[]{:S(2)}) async-start(), calls=%async_computation.3 | async-start | bytes 2097152 | tf_op jit(solution)/shard_map/psum | solution.py:71
  32.9 3.5 %copy-start = (bf16[512,1024]{1,0:T(8,128)(2,1)S(1)}, bf16[512,1024]{1,0:T(8,128)(2,1)}, u32[]{:S(2)}) copy-start(bf16[512,1024]{1,0:T(8,128)(2,1)} %all-gather.2.cloned.1.call-done) | copy-start | bytes 3145732
  37.9 74.6 %reduce-scatter.3.cloned.1.call-start = ((), (), s32[]{:S(2)}) async-start(), calls=%async_computation.4 | async-start | bytes 393216 | tf_op jit(solution)/shard_map/reduce_scatter | solution.py:81
  105.7 33.6 %copy-start.1 = (u32[32]{0:T(128)S(1)}, u32[32]{0:T(128)}, u32[]{:S(2)}) copy-start(u32[32]{0:T(128)} %constant.62) | copy-start | bytes 388
  105.7 66.3 %reduce-scatter.5.cloned.1.call-start = ((), (), s32[]{:S(2)}) async-start(), calls=%async_computation.5 | async-start | bytes 3145728 | tf_op jit(solution)/shard_map/reduce_scatter | solution.py:87
  113.4 5.5 %collective-permute-start = (bf16[32,1024]{1,0:T(8,128)(2,1)S(1)}, bf16[32,1024]{1,0:T(8,128)(2,1)S(1)}, u32[]{:S(2)}, u32[]{:S(2)}) collective-permute-start(bf16[32,1024]{1,0:T(8,128)(2,1)S(1)} %convert_element_type.23), channel_id=1, source_target_pairs={{0,1},{1,4},{4,5},{5,8},{8,9},{9,12},{12,13},{13,0},{2,3},{3,6},{6... | collective-permute-start | bytes 196616 | tf_op jit(solution)/shard_map/ppermute | solution.py:27
  119.0 5.9 %collective-permute-start.1 = (bf16[32,1024]{1,0:T(8,128)(2,1)S(1)}, bf16[32,1024]{1,0:T(8,128)(2,1)S(1)}, u32[]{:S(2)}, u32[]{:S(2)}) collective-permute-start(bf16[32,1024]{1,0:T(8,128)(2,1)S(1)} %collective-permute-done), channel_id=1, source_target_pairs={{0,1},{1,4},{4,5},{5,8},{8,9},{9,12},{12,13},{13,0},{2,3},{3,6},{6... | collective-permute-start | bytes 196616 | tf_op jit(solution)/shard_map/ppermute | solution.py:27
  119.0 5.9 %collective-permute-start.4 = (bf16[32,1024]{1,0:T(8,128)(2,1)S(1)}, bf16[32,1024]{1,0:T(8,128)(2,1)S(1)}, u32[]{:S(2)}, u32[]{:S(2)}) collective-permute-start(bf16[32,1024]{1,0:T(8,128)(2,1)S(1)} %convert_element_type.23), channel_id=1, source_target_pairs={{1,0},{4,1},{5,4},{8,5},{9,8},{12,9},{13,12},{0,13},{3,2},{6,3},{7... | collective-permute-start | bytes 196616 | tf_op jit(solution)/shard_map/ppermute | solution.py:30
  124.9 5.5 %collective-permute-start.2 = (bf16[32,1024]{1,0:T(8,128)(2,1)S(1)}, bf16[32,1024]{1,0:T(8,128)(2,1)S(1)}, u32[]{:S(2)}, u32[]{:S(2)}) collective-permute-start(bf16[32,1024]{1,0:T(8,128)(2,1)S(1)} %collective-permute-done.1), channel_id=1, source_target_pairs={{0,1},{1,4},{4,5},{5,8},{8,9},{9,12},{12,13},{13,0},{2,3},{3,6},{6... | collective-permute-start | bytes 196616 | tf_op jit(solution)/shard_map/ppermute | solution.py:27
  124.9 5.5 %collective-permute-start.5 = (bf16[32,1024]{1,0:T(8,128)(2,1)S(1)}, bf16[32,1024]{1,0:T(8,128)(2,1)S(1)}, u32[]{:S(2)}, u32[]{:S(2)}) collective-permute-start(bf16[32,1024]{1,0:T(8,128)(2,1)S(1)} %collective-permute-done.4), channel_id=1, source_target_pairs={{1,0},{4,1},{5,4},{8,5},{9,8},{12,9},{13,12},{0,13},{3,2},{6,3},{7... | collective-permute-start | bytes 196616 | tf_op jit(solution)/shard_map/ppermute | solution.py:30
  130.4 5.5 %collective-permute-start.3 = (bf16[32,1024]{1,0:T(8,128)(2,1)S(1)}, bf16[32,1024]{1,0:T(8,128)(2,1)S(1)}, u32[]{:S(2)}, u32[]{:S(2)}) collective-permute-start(bf16[32,1024]{1,0:T(8,128)(2,1)S(1)} %collective-permute-done.2), channel_id=1, source_target_pairs={{0,1},{1,4},{4,5},{5,8},{8,9},{9,12},{12,13},{13,0},{2,3},{3,6},{6... | collective-permute-start | bytes 196616 | tf_op jit(solution)/shard_map/ppermute | solution.py:27
  130.4 6.5 %collective-permute-start.6 = (bf16[32,1024]{1,0:T(8,128)(2,1)S(1)}, bf16[32,1024]{1,0:T(8,128)(2,1)S(1)}, u32[]{:S(2)}, u32[]{:S(2)}) collective-permute-start(bf16[32,1024]{1,0:T(8,128)(2,1)S(1)} %collective-permute-done.5), channel_id=1, source_target_pairs={{1,0},{4,1},{5,4},{8,5},{9,8},{12,9},{13,12},{0,13},{3,2},{6,3},{7... | collective-permute-start | bytes 196616 | tf_op jit(solution)/shard_map/ppermute | solution.py:30
Sparse Core Ops, SparseCore 0:
  8.9 23.9 all-gather.1
  38.0 58.8 all-reduce.2
  105.9 6.6 reduce-scatter.2
  139.4 32.5 reduce-scatter.4
